TPU v7x, 512 devices: a whole 4x8x8 slice. The times are simulated.
512 devices in a mesh: tok: 16 (over z, y_hi), hid: 32 (over y_lo, x, core).
Axes of the slice: x: 4, y: 8 (y_hi: 2, y_lo: 4; y = y_hi * 4 + y_lo), z: 8, core: 2. Of those that a mesh axis runs over, the one named last changes fastest.
Arguments:
- resid_in: bfloat16 [512, 8192], P('hid', 'tok'), may hold values from -64 to 64
- norm_gain: float32 [8192], P('tok'), may hold values from 0.1 to 1.9
- gate_weight: bfloat16 [8192, 28672], P('tok', 'hid'), may hold values from -0.0625 to 0.0625
- up_weight: bfloat16 [8192, 28672], P('tok', 'hid'), may hold values from -0.0625 to 0.0625
- down_weight: bfloat16 [28672, 8192], P('hid', 'tok'), may hold values from -0.0625 to 0.0625
- labels: int32 [512], replicated, may hold values from 0 to 63
Outputs:
- gram: float32 [8192, 8192], P(('tok', 'hid'))
- cross: float32 [8192, 64], P(('tok', 'hid'))
All inputs are finite; a program needn't handle non-finite values.
Results may differ from a plain program's by a relative error of at most 0.014.
Values may be sent and summed in bfloat16 or wider, within the bound.
A program may use at most 64 MiB of HBM per device.

v0:
```python
import jax
import jax.numpy as jnp
from jax import lax
from jax.sharding import PartitionSpec as P

D = 8192
CLASSES = 64


def on_device(resid_in, norm_gain, gate_weight, up_weight, down_weight, labels):
    gathered = lax.all_gather(resid_in, "hid", axis=0, tiled=True)
    xf = gathered.astype(jnp.float32)
    local_sq = jnp.sum(xf * xf, axis=1)
    total_sq = lax.psum(local_sq, "tok")
    scale_rows = lax.rsqrt(total_sq / float(D) + 1e-05)
    normed = (xf * scale_rows[:, None] * norm_gain[None, :]).astype(jnp.bfloat16)
    both_weights = jnp.concatenate([gate_weight, up_weight], axis=1)
    shard_ff = gate_weight.shape[1]
    paired = lax.psum_scatter(
        jnp.dot(normed, both_weights, preferred_element_type=jnp.float32).astype(jnp.bfloat16),
        "tok",
        scatter_dimension=0,
        tiled=True,
    ).astype(jnp.float32)
    hidden = (jax.nn.silu(paired[:, :shard_ff]) * paired[:, shard_ff:]).astype(jnp.bfloat16)
    partial_out = jnp.dot(
        lax.all_gather(hidden, "tok", axis=0, tiled=True),
        down_weight,
        preferred_element_type=jnp.float32,
    )
    ntok = xf.shape[0]
    panel = xf.shape[1] // lax.axis_size("hid")
    offset = lax.axis_index("hid") * panel
    summed = lax.psum_scatter(
        partial_out.astype(jnp.bfloat16), "hid", scatter_dimension=1, tiled=True
    ).astype(jnp.float32)
    x_cols = lax.dynamic_slice_in_dim(xf, offset, panel, 1)
    resid_cols = (x_cols + summed).astype(jnp.bfloat16)
    prod = lax.dot_general(
        resid_cols,
        lax.all_gather(resid_cols, ("tok", "hid"), axis=1, tiled=True),
        (((0,), (0,)), ((), ())),
        preferred_element_type=jnp.float32,
    )
    gram = prod / float(ntok)
    onehot = (labels[:, None] == jnp.arange(CLASSES, dtype=jnp.int32)[None, :]).astype(jnp.bfloat16)
    counts = jnp.sum(onehot.astype(jnp.float32), axis=0)
    class_sums = lax.dot_general(
        resid_cols, onehot, (((0,), (0,)), ((), ())), preferred_element_type=jnp.float32
    )
    cross = class_sums / jnp.maximum(counts, 1.0)[None, :]
    return (gram, cross)


def solution(mesh):
    return jax.shard_map(
        on_device,
        mesh=mesh,
        in_specs=(
            P("hid", "tok"),
            P("tok"),
            P("tok", "hid"),
            P("tok", "hid"),
            P("hid", "tok"),
            P(),
        ),
        out_specs=(P(("tok", "hid"), None), P(("tok", "hid"), None)),
        check_vma=False,
    )
```

profile of v0, /device:TPU:1, one launch (start us, length us, event | category | flops | bytes accessed | tf_op | source)
XLA Modules:
  0.0 691.0 jit_solution(11875496450596271961)
XLA Ops:
  7.2 0.0 copy-start
  7.2 0.0 reduce-scatter.3.cloned.1.call-start
  7.2 46.5 %all_gather.9 = bf16[512,512]{1,0:T(8,128)(2,1)S(1)} all-gather(bf16[16,512]{1,0:T(8,128)(2,1)} %param.6), channel_id=1, replica_groups=mesh['tok'=16,'hid'=32] {'hid'}, dimensions={0}, use_global_device_ids=true | all-gather | bytes 540672 | tf_op jit(solution)/shard_map/all_gather | solution.py:11
  53.7 0.2 copy.10
  53.9 0.2 multiply_reduce_fusion
  54.1 50.9 %psum.7 = f32[512]{0:T(512)S(1)} all-reduce(f32[512]{0:T(512)S(1)} %multiply_reduce_fusion), channel_id=1, replica_groups=mesh['tok'=16,'hid'=32] {'tok'}, use_global_device_ids=true, to_apply=%region_1.0 | all-reduce | flops 512 | bytes 4096 | tf_op jit(solution)/shard_map/psum | solution.py:14
  105.0 4.0 convolution_convert_fusion
  109.0 0.0 reduce-scatter.3.cloned.1.call-update
  109.0 0.0 copy-start.1
  109.0 0.0 reduce-scatter.5.cloned.1.call-start
  109.0 217.4 %reduce-scatter.3.cloned.1.call-done = bf16[32,1792]{1,0:T(8,128)(2,1)} async-done(((bf16[512,1792]{1,0:T(8,128)(2,1)}), bf16[32,1792]{1,0:T(8,128)(2,1)}) %reduce-scatter.3.cloned.1.call-update) | async-done | bytes 114704 | tf_op jit(solution)/shard_map/reduce_scatter | solution.py:19
  326.4 0.9 convert_element_type.33
  327.4 57.8 %all_gather.10 = bf16[512,896]{1,0:T(8,128)(2,1)S(1)} all-gather(bf16[32,896]{1,0:T(8,128)(2,1)S(1)} %fusion.7), channel_id=1, replica_groups=mesh['tok'=16,'hid'=32] {'tok'}, dimensions={0}, use_global_device_ids=true | all-gather | bytes 974848 | tf_op jit(solution)/shard_map/all_gather | solution.py:27
  385.2 1.6 convolution_convert_fusion.1
  386.7 0.0 reduce-scatter.5.cloned.1.call-update
  386.7 0.0 all-gather.2.cloned.1.call-start
  386.8 0.1 convert_element_type.30
  386.9 157.9 %reduce-scatter.5.cloned.1.call-done = bf16[512,16]{0,1:T(8,128)(2,1)} async-done(((bf16[512,512]{0,1:T(8,128)(2,1)}), bf16[512,16]{0,1:T(8,128)(2,1)}) %reduce-scatter.5.cloned.1.call-update) | async-done | bytes 16400 | tf_op jit(solution)/shard_map/reduce_scatter | solution.py:34
  544.9 1.3 add_convert_fusion
  546.2 0.0 all-gather.2.cloned.1.call-update
  546.2 0.1 convert_reduce_fusion
  546.3 1.5 convolution_divide_fusion
  547.8 130.1 %all-gather.2.cloned.1.call-done = bf16[512,8192]{0,1:T(8,128)(2,1)} async-done(((bf16[512,16]{0,1:T(8,128)(2,1)}), bf16[512,8192]{0,1:T(8,128)(2,1)}) %all-gather.2.cloned.1.call-update) | async-done | bytes 8388624 | tf_op jit(solution)/shard_map/all_gather | solution.py:41
  677.9 6.5 convolution_multiply_fusion
  (5 shorter events, 0.1 us)
Async XLA Ops:
  7.2 378.0 %copy-start = (bf16[896,512]{1,0:T(8,128)(2,1)S(1)}, bf16[896,512]{1,0:T(8,128)(2,1)}, u32[]{:S(2)}) copy-start(bf16[896,512]{1,0:T(8,128)(2,1)} %param.10) | copy-start | bytes 2752516
  7.2 319.2 %reduce-scatter.3.cloned.1.call-start = ((), (), s32[]{:S(2)}) async-start(), calls=%async_computation.2 | async-start | bytes 1949696 | tf_op jit(solution)/shard_map/reduce_scatter | solution.py:19
  109.0 437.2 %copy-start.1 = (s32[512]{0:T(512)S(1)}, s32[512]{0:T(512)}, u32[]{:S(2)}) copy-start(s32[512]{0:T(512)} %param.11) | copy-start | bytes 6148
  109.0 435.9 %reduce-scatter.5.cloned.1.call-start = ((), (), s32[]{:S(2)}) async-start(), calls=%async_computation.3 | async-start | bytes 540672 | tf_op jit(solution)/shard_map/reduce_scatter | solution.py:34
  386.7 291.2 %all-gather.2.cloned.1.call-start = ((), (), s32[]{:S(2)}) async-start(), calls=%async_computation.4 | async-start | bytes 8404992 | tf_op jit(solution)/shard_map/all_gather | solution.py:41
Sparse Core Ops, SparseCore 0:
  109.1 217.2 reduce-scatter.2
  386.9 157.9 reduce-scatter.4
  549.3 128.5 all-gather.1
where the time goes:
time: 691 us
  waiting for transfers between devices  505 us (73%)
  blocking collectives  155 us (22%)
  between operations  13.8 us (2%)
  matrix products  13.5 us (2%)
    reduce_scatter x1, waiting for transfers between devices, on_device(): lax.psum_scatter(jnp.dot(normed, both_weights, preferred_element_type=jnp...  217 us
    reduce_scatter x1, waiting for transfers between devices, on_device(): lax.psum_scatter(partial_out.astype(jnp.bfloat16), 'hid', scatter_dimensi...  158 us
    all_gather x1, waiting for transfers between devices, on_device(): lax.all_gather(resid_cols, ('tok', 'hid'), axis=1, tiled=True)  130 us
    all_gather x1, blocking collectives, on_device(): lax.all_gather(hidden, 'tok', axis=0, tiled=True)  57.8 us
    psum x1, blocking collectives, on_device(): total_sq = lax.psum(local_sq, 'tok')  50.9 us
    all_gather x1, blocking collectives, on_device(): gathered = lax.all_gather(resid_in, 'hid', axis=0, tiled=True)  46.5 us
  transfers between devices with their start and end apart: 3, of which 3 were waited for; matrix products, arithmetic and copies ran while one was open for 0% of the time, Pallas kernels for 0%

commit v1 on v0

--- a/solution.py
+++ b/solution.py
@@ -11,7 +11,7 @@
     gathered = lax.all_gather(resid_in, "hid", axis=0, tiled=True)
     xf = gathered.astype(jnp.float32)
     local_sq = jnp.sum(xf * xf, axis=1)
-    total_sq = lax.psum(local_sq, "tok")
+    total_sq = jnp.sum(lax.all_gather(local_sq, "tok"), axis=0)
     scale_rows = lax.rsqrt(total_sq / float(D) + 1e-05)
     normed = (xf * scale_rows[:, None] * norm_gain[None, :]).astype(jnp.bfloat16)
     both_weights = jnp.concatenate([gate_weight, up_weight], axis=1)

time: 691 us -> 689 us (level)
    psum x1 -> x0, blocking collectives: 50.9 us -> none  [on_device(): total_sq = lax.psum(local_sq, 'tok')]
    all_gather x0 -> x1, blocking collectives: none -> 49.9 us  [on_device(): total_sq = jnp.sum(lax.all_gather(local_sq, 'tok'), axis=0)]
where the time goes in v1:
time: 689 us; the launch traced here: 688 us
  waiting for transfers between devices  506 us (73%)
  blocking collectives  152 us (22%)
  between operations  13.8 us (2%)
  matrix products  13.5 us (2%)
    reduce_scatter x1, waiting for transfers between devices, on_device(): lax.psum_scatter(jnp.dot(normed, both_weights, preferred_element_type=jnp...  217 us
    reduce_scatter x1, waiting for transfers between devices, on_device(): lax.psum_scatter(partial_out.astype(jnp.bfloat16), 'hid', scatter_dimensi...  159 us
    all_gather x1, waiting for transfers between devices, on_device(): lax.all_gather(resid_cols, ('tok', 'hid'), axis=1, tiled=True)  130 us
    all_gather x1, blocking collectives, on_device(): lax.all_gather(hidden, 'tok', axis=0, tiled=True)  55.4 us
    all_gather x1, blocking collectives, on_device(): total_sq = jnp.sum(lax.all_gather(local_sq, 'tok'), axis=0)  49.9 us
    all_gather x1, blocking collectives, on_device(): gathered = lax.all_gather(resid_in, 'hid', axis=0, tiled=True)  46.5 us
  transfers between devices with their start and end apart: 3, of which 3 were waited for; matrix products, arithmetic and copies ran while one was open for 0% of the time, Pallas kernels for 0%

profile of v1, /device:TPU:1, one launch (start us, length us, event | category | flops | bytes accessed | tf_op | source)
XLA Modules:
  0.0 688.3 jit_solution(2523648044745776266)
XLA Ops:
  7.2 0.0 copy-start
  7.2 0.0 reduce-scatter.3.cloned.1.call-start
  7.2 46.5 %all_gather.15 = bf16[512,512]{1,0:T(8,128)(2,1)S(1)} all-gather(bf16[16,512]{1,0:T(8,128)(2,1)} %param.6), channel_id=1, replica_groups=mesh['tok'=16,'hid'=32] {'hid'}, dimensions={0}, use_global_device_ids=true | all-gather | bytes 540672 | tf_op jit(solution)/shard_map/all_gather | solution.py:11
  53.7 0.2 copy.10
  53.9 0.2 multiply_reduce_fusion
  54.1 49.9 %all-gather.1 = f32[16,1,512]{2,1,0:T(1,128)S(1)} all-gather(f32[1,1,512]{2,1,0:T(1,128)S(1)} %bitcast.6), channel_id=2, replica_groups=mesh['tok'=16,'hid'=32] {'tok'}, dimensions={0}, use_global_device_ids=true | all-gather | bytes 34816 | tf_op jit(solution)/shard_map/all_gather | solution.py:14
  104.0 4.0 convolution_convert_fusion
  108.0 0.0 reduce-scatter.3.cloned.1.call-update
  108.0 0.0 copy-start.1
  108.0 0.0 reduce-scatter.5.cloned.1.call-start
  108.1 217.3 %reduce-scatter.3.cloned.1.call-done = bf16[32,1792]{1,0:T(8,128)(2,1)} async-done(((bf16[512,1792]{1,0:T(8,128)(2,1)}), bf16[32,1792]{1,0:T(8,128)(2,1)}) %reduce-scatter.3.cloned.1.call-update) | async-done | bytes 114704 | tf_op jit(solution)/shard_map/reduce_scatter | solution.py:19
  325.4 0.9 convert_element_type.33
  326.3 55.4 %all_gather.18 = bf16[512,896]{1,0:T(8,128)(2,1)S(1)} all-gather(bf16[32,896]{1,0:T(8,128)(2,1)S(1)} %fusion.7), channel_id=1, replica_groups=mesh['tok'=16,'hid'=32] {'tok'}, dimensions={0}, use_global_device_ids=true | all-gather | bytes 974848 | tf_op jit(solution)/shard_map/all_gather | solution.py:27
  381.8 1.6 convolution_convert_fusion.1
  383.3 0.0 reduce-scatter.5.cloned.1.call-update
  383.3 0.0 all-gather.4.cloned.1.call-start
  383.4 0.1 convert_element_type.30
  383.5 158.7 %reduce-scatter.5.cloned.1.call-done = bf16[512,16]{0,1:T(8,128)(2,1)} async-done(((bf16[512,512]{0,1:T(8,128)(2,1)}), bf16[512,16]{0,1:T(8,128)(2,1)}) %reduce-scatter.5.cloned.1.call-update) | async-done | bytes 16400 | tf_op jit(solution)/shard_map/reduce_scatter | solution.py:34
  542.3 1.3 add_convert_fusion
  543.6 0.0 all-gather.4.cloned.1.call-update
  543.6 0.1 convert_reduce_fusion
  543.7 1.5 convolution_divide_fusion
  545.2 130.1 %all-gather.4.cloned.1.call-done = bf16[512,8192]{0,1:T(8,128)(2,1)} async-done(((bf16[512,16]{0,1:T(8,128)(2,1)}), bf16[512,8192]{0,1:T(8,128)(2,1)}) %all-gather.4.cloned.1.call-update) | async-done | bytes 8388624 | tf_op jit(solution)/shard_map/all_gather | solution.py:41
  675.3 6.5 convolution_multiply_fusion
  (6 shorter events, 0.1 us)
Async XLA Ops:
  7.2 374.6 %copy-start = (bf16[896,512]{1,0:T(8,128)(2,1)S(1)}, bf16[896,512]{1,0:T(8,128)(2,1)}, u32[]{:S(2)}) copy-start(bf16[896,512]{1,0:T(8,128)(2,1)} %param.10) | copy-start | bytes 2752516
  7.2 318.2 %reduce-scatter.3.cloned.1.call-start = ((), (), s32[]{:S(2)}) async-start(), calls=%async_computation.2 | async-start | bytes 1949696 | tf_op jit(solution)/shard_map/reduce_scatter | solution.py:19
  108.0 435.6 %copy-start.1 = (s32[512]{0:T(512)S(1)}, s32[512]{0:T(512)}, u32[]{:S(2)}) copy-start(s32[512]{0:T(512)} %param.11) | copy-start | bytes 6148
  108.0 434.2 %reduce-scatter.5.cloned.1.call-start = ((), (), s32[]{:S(2)}) async-start(), calls=%async_computation.3 | async-start | bytes 540672 | tf_op jit(solution)/shard_map/reduce_scatter | solution.py:34
  383.3 292.0 %all-gather.4.cloned.1.call-start = ((), (), s32[]{:S(2)}) async-start(), calls=%async_computation.4 | async-start | bytes 8404992 | tf_op jit(solution)/shard_map/all_gather | solution.py:41
Sparse Core Ops, SparseCore 0:
  108.2 217.1 reduce-scatter.2
  383.5 158.7 reduce-scatter.4
  546.7 128.5 all-gather.3

commit v2 on v0

--- a/solution.py
+++ b/solution.py
@@ -38,7 +38,12 @@
     resid_cols = (x_cols + summed).astype(jnp.bfloat16)
     prod = lax.dot_general(
         resid_cols,
-        lax.all_gather(resid_cols, ("tok", "hid"), axis=1, tiled=True),
+        jnp.concatenate(
+            lax.all_to_all(
+                jnp.stack([resid_cols] * lax.axis_size(("tok", "hid"))), ("tok", "hid"), 0, 0
+            ),
+            axis=1,
+        ),
         (((0,), (0,)), ((), ())),
         preferred_element_type=jnp.float32,
     )

time: 691 us -> 767 us (1.11)
  waiting for transfers between devices: 505 us -> 560 us
  starting transfers between devices: 0.12 us -> 19.3 us
    all_to_all x0 -> x1, waiting for transfers between devices: none -> 185 us  [on_device(): lax.all_to_all(jnp.stack([resid_cols] * lax.axis_size(('tok', 'hid'))), (...]
    all_gather x1 -> x0, waiting for transfers between devices: 130 us -> none  [on_device(): lax.all_gather(resid_cols, ('tok', 'hid'), axis=1, tiled=True)]
    all_to_all x0 -> x1, starting transfers between devices: none -> 19.2 us  [on_device(): lax.all_to_all(jnp.stack([resid_cols] * lax.axis_size(('tok', 'hid'))), (...]
where the time goes in v2:
time: 767 us
  waiting for transfers between devices  560 us (73%)
  blocking collectives  155 us (20%)
  starting transfers between devices  19.3 us (3%)
  between operations  14.1 us (2%)
  matrix products  12.7 us (2%)
    reduce_scatter x1, waiting for transfers between devices, on_device(): lax.psum_scatter(jnp.dot(normed, both_weights, preferred_element_type=jnp...  217 us
    all_to_all x1, waiting for transfers between devices, on_device(): lax.all_to_all(jnp.stack([resid_cols] * lax.axis_size(('tok', 'hid'))), (...  185 us
    reduce_scatter x1, waiting for transfers between devices, on_device(): lax.psum_scatter(partial_out.astype(jnp.bfloat16), 'hid', scatter_dimensi...  157 us
    all_gather x1, blocking collectives, on_device(): lax.all_gather(hidden, 'tok', axis=0, tiled=True)  57.1 us
    psum x1, blocking collectives, on_device(): total_sq = lax.psum(local_sq, 'tok')  50.9 us
    all_gather x1, blocking collectives, on_device(): gathered = lax.all_gather(resid_in, 'hid', axis=0, tiled=True)  46.5 us
    all_to_all x1, starting transfers between devices, on_device(): lax.all_to_all(jnp.stack([resid_cols] * lax.axis_size(('tok', 'hid'))), (...  19.2 us
  transfers between devices with their start and end apart: 3, of which 3 were waited for; matrix products, arithmetic and copies ran while one was open for 0% of the time, Pallas kernels for 0%

profile of v2, /device:TPU:1, one launch (start us, length us, event | category | flops | bytes accessed | tf_op | source)
XLA Modules:
  0.0 767.1 jit_solution(6145148521660917136)
XLA Ops:
  7.2 0.0 copy-start
  7.2 0.0 reduce-scatter.3.cloned.1.call-start
  7.2 46.5 %all_gather.6 = bf16[512,512]{1,0:T(8,128)(2,1)S(1)} all-gather(bf16[16,512]{1,0:T(8,128)(2,1)} %param.6), channel_id=1, replica_groups=mesh['tok'=16,'hid'=32] {'hid'}, dimensions={0}, use_global_device_ids=true | all-gather | bytes 540672 | tf_op jit(solution)/shard_map/all_gather | solution.py:11
  53.7 0.2 copy.12
  53.9 0.2 multiply_reduce_fusion
  54.1 50.9 %psum.7 = f32[512]{0:T(512)S(1)} all-reduce(f32[512]{0:T(512)S(1)} %multiply_reduce_fusion), channel_id=1, replica_groups=mesh['tok'=16,'hid'=32] {'tok'}, use_global_device_ids=true, to_apply=%region_1.0 | all-reduce | flops 512 | bytes 4096 | tf_op jit(solution)/shard_map/psum | solution.py:14
  105.0 4.0 convolution_convert_fusion
  109.0 0.0 reduce-scatter.3.cloned.1.call-update
  109.0 0.0 reduce-scatter.5.cloned.1.call-start
  109.0 217.5 %reduce-scatter.3.cloned.1.call-done = bf16[32,1792]{1,0:T(8,128)(2,1)} async-done(((bf16[512,1792]{1,0:T(8,128)(2,1)}), bf16[32,1792]{1,0:T(8,128)(2,1)}) %reduce-scatter.3.cloned.1.call-update) | async-done | bytes 114704 | tf_op jit(solution)/shard_map/reduce_scatter | solution.py:19
  326.5 0.9 convert_element_type.33
  327.5 57.1 %all_gather.7 = bf16[512,896]{1,0:T(8,128)(2,1)S(1)} all-gather(bf16[32,896]{1,0:T(8,128)(2,1)S(1)} %fusion.7), channel_id=1, replica_groups=mesh['tok'=16,'hid'=32] {'tok'}, dimensions={0}, use_global_device_ids=true | all-gather | bytes 974848 | tf_op jit(solution)/shard_map/all_gather | solution.py:27
  384.6 0.0 copy-done
  384.6 1.6 convolution_convert_fusion.1
  386.2 0.0 reduce-scatter.5.cloned.1.call-update
  386.2 0.1 convert_element_type.30
  386.4 157.0 %reduce-scatter.5.cloned.1.call-done = bf16[512,16]{0,1:T(8,128)(2,1)} async-done(((bf16[512,512]{0,1:T(8,128)(2,1)}), bf16[512,16]{0,1:T(8,128)(2,1)}) %reduce-scatter.5.cloned.1.call-update) | async-done | bytes 16400 | tf_op jit(solution)/shard_map/reduce_scatter | solution.py:34
  543.4 0.7 add_convert_fusion
  544.1 4.3 stack.2
  548.4 19.2 %all-to-all-start = ((bf16[512,512,16]{1,2,0:T(8,128)(2,1)}), bf16[512,512,16]{1,2,0:T(8,128)(2,1)}, u32[]{:S(2)}, u32[]{:S(2)}) async-start(bf16[512,512,16]{1,2,0:T(8,128)(2,1)} %stack.2), calls=%async_computation.2 | async-start | bytes 16777216 | tf_op jit(solution)/shard_map/all_to_all | solution.py:42
  567.7 0.1 convert_reduce_fusion
  567.8 0.7 convolution_divide_fusion
  568.5 185.2 %all-to-all-done = bf16[512,512,16]{1,2,0:T(8,128)(2,1)} async-done(((bf16[512,512,16]{1,2,0:T(8,128)(2,1)}), bf16[512,512,16]{1,2,0:T(8,128)(2,1)}, u32[]{:S(2)}, u32[]{:S(2)}) %all-to-all-start) | async-done | bytes 8388640 | tf_op jit(solution)/shard_map/all_to_all | solution.py:42
  753.8 6.5 convolution_multiply_fusion
  (5 shorter events, 0.1 us)
Async XLA Ops:
  7.2 377.5 %copy-start = (bf16[896,512]{1,0:T(8,128)(2,1)S(1)}, bf16[896,512]{1,0:T(8,128)(2,1)}, u32[]{:S(2)}) copy-start(bf16[896,512]{1,0:T(8,128)(2,1)} %param.10) | copy-start | bytes 2752516
  7.2 319.3 %reduce-scatter.3.cloned.1.call-start = ((), (), s32[]{:S(2)}) async-start(), calls=%async_computation.3 | async-start | bytes 1949696 | tf_op jit(solution)/shard_map/reduce_scatter | solution.py:19
  109.0 434.4 %reduce-scatter.5.cloned.1.call-start = ((), (), s32[]{:S(2)}) async-start(), calls=%async_computation.4 | async-start | bytes 540672 | tf_op jit(solution)/shard_map/reduce_scatter | solution.py:34
  548.4 19.3 %copy-start.1 = (s32[512]{0:T(512)S(1)}, s32[512]{0:T(512)}, u32[]{:S(2)}) copy-start(s32[512]{0:T(512)} %param.11) | copy-start | bytes 6148
  548.4 205.4 %all-to-all-start = ((bf16[512,512,16]{1,2,0:T(8,128)(2,1)}), bf16[512,512,16]{1,2,0:T(8,128)(2,1)}, u32[]{:S(2)}, u32[]{:S(2)}) async-start(bf16[512,512,16]{1,2,0:T(8,128)(2,1)} %stack.2), calls=%async_computation.2 | async-start | bytes 16777216 | tf_op jit(solution)/shard_map/all_to_all | solution.py:42
Sparse Core Ops, SparseCore 0:
  109.1 217.3 reduce-scatter.2
  386.3 157.0 reduce-scatter.4
